TPU v7x, 32 devices: a whole 2x2x4 slice. The times are simulated.
32 devices in a mesh: dp: 16 (over z, y, core), seq: 2 (over x).
Axes of the slice: x: 2, y: 2, z: 4, core: 2. Of those that a mesh axis runs over, the one named last changes fastest.
Arguments:
- latents: float32 [16, 256, 1152], P('dp', 'seq'), may hold values from -6 to 6
- condition: float32 [8, 1152], replicated, may hold values from -6 to 6
- slot_latent: int32 [16, 1], P('dp'), may hold values from 0 to 7, as said below
- slot_counts: int32 [16], P('dp'), may hold values from 0 to 1, as said below
- output_gradient: float32 [16, 256, 1152], P('dp', 'seq'), may hold values from -6 to 6
- ada_weight: float32 [1152, 6912], P(None, ('dp', 'seq')), may hold values from -0.1875 to 0.1875
- ada_bias: float32 [6912], P(('dp', 'seq')), may hold values from -1.75 to 1.75
- qkv_weight: float32 [1152, 3456], P('dp', 'seq'), may hold values from -5 to 5, as said below
- qkv_bias: float32 [3456], P('seq'), may hold values from -1.25 to 1.25
- out_weight: float32 [1152, 1152], P('dp', 'seq'), may hold values from -0.75 to 0.75
- out_bias: float32 [1152], P('seq'), may hold values from -1.25 to 1.25
- up_weight: float32 [1152, 4608], P('dp', 'seq'), may hold values from -0.1875 to 0.1875
- up_bias: float32 [4608], P('seq'), may hold values from -1.25 to 1.25
- down_weight: float32 [4608, 1152], P('dp', 'seq'), may hold values from -0.09375 to 0.09375
- down_bias: float32 [1152], P('seq'), may hold values from -1.25 to 1.25
- mean_adaw: float32 [1152, 6912], P(None, ('dp', 'seq')), may hold values from -16 to 16
- mean_adab: float32 [6912], P(('dp', 'seq')), may hold values from -16 to 16
- mean_qkvw: float32 [1152, 3456], P('dp', 'seq'), may hold values from -16 to 16
- mean_qkvb: float32 [3456], P('seq'), may hold values from -16 to 16
- mean_outw: float32 [1152, 1152], P('dp', 'seq'), may hold values from -16 to 16
- mean_outb: float32 [1152], P('seq'), may hold values from -16 to 16
- mean_upw: float32 [1152, 4608], P('dp', 'seq'), may hold values from -16 to 16
- mean_upb: float32 [4608], P('seq'), may hold values from -16 to 16
- mean_downw: float32 [4608, 1152], P('dp', 'seq'), may hold values from -16 to 16
- mean_downb: float32 [1152], P('seq'), may hold values from -16 to 16
- sqmean_adaw: float32 [1152, 6912], P(None, ('dp', 'seq')), may hold values from 0.3 to 3
- sqmean_adab: float32 [6912], P(('dp', 'seq')), may hold values from 0.3 to 3
- sqmean_qkvw: float32 [1152, 3456], P('dp', 'seq'), may hold values from 0.3 to 3
- sqmean_qkvb: float32 [3456], P('seq'), may hold values from 0.3 to 3
- sqmean_outw: float32 [1152, 1152], P('dp', 'seq'), may hold values from 0.3 to 3
- sqmean_outb: float32 [1152], P('seq'), may hold values from 0.3 to 3
- sqmean_upw: float32 [1152, 4608], P('dp', 'seq'), may hold values from 0.3 to 3
- sqmean_upb: float32 [4608], P('seq'), may hold values from 0.3 to 3
- sqmean_downw: float32 [4608, 1152], P('dp', 'seq'), may hold values from 0.3 to 3
- sqmean_downb: float32 [1152], P('seq'), may hold values from 0.3 to 3
Outputs:
- block_output: float32 [16, 256, 1152], P('dp', 'seq')
- latent_gradient: float32 [16, 256, 1152], P('dp', 'seq')
- condition_grad: float32 [8, 1152], replicated
- grad_adaw: float32 [1152, 6912], P(None, ('dp', 'seq'))
- grad_adab: float32 [6912], P(('dp', 'seq'))
- grad_qkvw: float32 [1152, 3456], P('dp', 'seq')
- grad_qkvb: float32 [3456], P('seq')
- grad_outw: float32 [1152, 1152], P('dp', 'seq')
- grad_outb: float32 [1152], P('seq')
- grad_upw: float32 [1152, 4608], P('dp', 'seq')
- grad_upb: float32 [4608], P('seq')
- grad_downw: float32 [4608, 1152], P('dp', 'seq')
- grad_downb: float32 [1152], P('seq')
- newval_adaw: float32 [1152, 6912], P(None, ('dp', 'seq'))
- newval_adab: float32 [6912], P(('dp', 'seq'))
- newval_qkvw: float32 [1152, 3456], P('dp', 'seq')
- newval_qkvb: float32 [3456], P('seq')
- newval_outw: float32 [1152, 1152], P('dp', 'seq')
- newval_outb: float32 [1152], P('seq')
- newval_upw: float32 [1152, 4608], P('dp', 'seq')
- newval_upb: float32 [4608], P('seq')
- newval_downw: float32 [4608, 1152], P('dp', 'seq')
- newval_downb: float32 [1152], P('seq')
- newmean_adaw: float32 [1152, 6912], P(None, ('dp', 'seq'))
- newmean_adab: float32 [6912], P(('dp', 'seq'))
- newmean_qkvw: float32 [1152, 3456], P('dp', 'seq')
- newmean_qkvb: float32 [3456], P('seq')
- newmean_outw: float32 [1152, 1152], P('dp', 'seq')
- newmean_outb: float32 [1152], P('seq')
- newmean_upw: float32 [1152, 4608], P('dp', 'seq')
- newmean_upb: float32 [4608], P('seq')
- newmean_downw: float32 [4608, 1152], P('dp', 'seq')
- newmean_downb: float32 [1152], P('seq')
- newsqr_adaw: float32 [1152, 6912], P(None, ('dp', 'seq'))
- newsqr_adab: float32 [6912], P(('dp', 'seq'))
- newsqr_qkvw: float32 [1152, 3456], P('dp', 'seq')
- newsqr_qkvb: float32 [3456], P('seq')
- newsqr_outw: float32 [1152, 1152], P('dp', 'seq')
- newsqr_outb: float32 [1152], P('seq')
- newsqr_upw: float32 [1152, 4608], P('dp', 'seq')
- newsqr_upb: float32 [4608], P('seq')
- newsqr_downw: float32 [4608, 1152], P('dp', 'seq')
- newsqr_downb: float32 [1152], P('seq')
Inputs may be any that keep to these rules, and one draw needn't show every extreme that they name: `slot_counts`: live slots of a group come first; the entries sum to 8; some group has all 1 slots live in every draw, some groups may have none. `slot_latent`: the live slots name every latent exactly once; entries of slots that are not live are arbitrary latents. `qkv_weight`: query and value columns have entries of order 1152^-1/2; key columns may have entries up to the ends of the range.
All inputs are finite; a program needn't handle non-finite values.
Results may differ from a plain program's by a relative error of at most 0.012.
The roundings to bfloat16 on the way count: a program that leaves them out, or rounds other values in their place, can miss the bound.
Values may be sent and summed in bfloat16 or wider, within the bound.
A program may use at most 192 MiB of HBM per device.

v0:
```python
import jax
import jax.numpy as jnp
from jax import lax
from jax.sharding import PartitionSpec as P

H = 16
HD = 72
STEP = 2
EPS_NORM = 1e-06
GELU_COEF = 0.7978845608
GELU_CUBE = 0.044715
BETA_ONE = 0.9
BETA_TWO = 0.999
LEARN_RATE = 0.05
EPS_ADAM = 1e-08


def rounded(values):
    return lax.optimization_barrier(values.astype(jnp.bfloat16)).astype(jnp.float32)


def normalize(values):
    center = values - jnp.mean(values, axis=-1, keepdims=True)
    spread = lax.rsqrt(jnp.mean(center * center, axis=-1, keepdims=True) + EPS_NORM)
    return (center * spread, spread)


def norm_back(upstream, normed, spread):
    return spread * (
        upstream
        - jnp.mean(upstream, axis=-1, keepdims=True)
        - normed * jnp.mean(upstream * normed, axis=-1, keepdims=True)
    )


def gelu_tanh(values):
    tanh_part = jnp.tanh(GELU_COEF * (values + GELU_CUBE * values * values * values))
    return 0.5 * values * (1.0 + tanh_part)


def gelu_slope(values):
    tanh_part = jnp.tanh(GELU_COEF * (values + GELU_CUBE * values * values * values))
    return 0.5 * (1.0 + tanh_part) + 0.5 * values * (1.0 - tanh_part * tanh_part) * GELU_COEF * (
        1.0 + 3.0 * GELU_CUBE * values * values
    )


def silu_slope(values):
    sigmoid_part = jax.nn.sigmoid(values)
    return sigmoid_part * (1.0 + values * (1.0 - sigmoid_part))


def adamw_step(parameter, gradient, first_mom, second):
    first_new = BETA_ONE * first_mom + (1.0 - BETA_ONE) * gradient
    second_new = BETA_TWO * second + (1.0 - BETA_TWO) * gradient * gradient
    first_hat = first_new / (1.0 - BETA_ONE**STEP)
    second_hat = second_new / (1.0 - BETA_TWO**STEP)
    return (
        parameter - LEARN_RATE * first_hat / (jnp.sqrt(second_hat) + EPS_ADAM),
        first_new,
        second_new,
    )


def collect(weight, bias):
    pieces, bias_full = (
        lax.all_gather(weight.astype(jnp.bfloat16), "seq", axis=1, tiled=True),
        lax.all_gather(bias.astype(jnp.bfloat16), "seq", axis=0, tiled=True),
    )
    return (lax.all_gather(pieces, "dp", axis=0, tiled=True), bias_full.astype(jnp.float32))


def collect_again(weight):
    pieces = lax.all_gather(weight.astype(jnp.bfloat16), "seq", axis=1, tiled=True)
    return lax.all_gather(pieces, "dp", axis=0, tiled=True)


def spread_grad(left, right):
    term = jnp.einsum("rc,rd->cd", left, right, preferred_element_type=jnp.float32)
    partial_value = lax.psum_scatter(term, "dp", scatter_dimension=0, tiled=True)
    return lax.psum_scatter(partial_value, "seq", scatter_dimension=1, tiled=True)


def on_device(
    latents,
    condition,
    slot_latent,
    slot_counts,
    output_gradient,
    ada_weight,
    ada_bias,
    qkv_weight,
    qkv_bias,
    out_weight,
    out_bias,
    up_weight,
    up_bias,
    down_weight,
    down_bias,
    mean_adaw,
    mean_adab,
    mean_qkvw,
    mean_qkvb,
    mean_outw,
    mean_outb,
    mean_upw,
    mean_upb,
    mean_downw,
    mean_downb,
    sqmean_adaw,
    sqmean_adab,
    sqmean_qkvw,
    sqmean_qkvb,
    sqmean_outw,
    sqmean_outb,
    sqmean_upw,
    sqmean_upb,
    sqmean_downw,
    sqmean_downb,
):
    slot_total, tok_dev, model_width = latents.shape
    row_count = slot_total * tok_dev
    scale = HD ** (-0.5)
    live_slots = jnp.arange(slot_total) < slot_counts[0]
    live_mask = live_slots[:, None, None]
    latent_count = condition.shape[0]
    slot_matches = (
        (slot_latent[0][:, None] == jnp.arange(latent_count)[None, :]) & live_slots[:, None]
    ).astype(jnp.float32)
    silu_cond = jax.nn.silu(condition).astype(jnp.bfloat16)
    mod_cols = jnp.dot(
        silu_cond, ada_weight.astype(jnp.bfloat16), preferred_element_type=jnp.float32
    ) + rounded(ada_bias)
    modulation = lax.all_gather(mod_cols, ("dp", "seq"), axis=1, tiled=True)
    slot_mod = jnp.dot(slot_matches, modulation, precision=lax.Precision.HIGHEST)[:, None, :]
    shift_att, scale_att, gate_att, shift_mlp, scale_mlp, gate_mlp = jnp.split(slot_mod, 6, axis=2)
    upstream = jnp.where(live_mask, output_gradient, 0.0)
    mat_qkv, vec_qkv = collect(qkv_weight, qkv_bias)
    normed_att, spread_att = normalize(latents)
    attn_in = (
        (normed_att * (1.0 + scale_att) + shift_att)
        .astype(jnp.bfloat16)
        .reshape(row_count, model_width)
    )
    qkv_all = (jnp.dot(attn_in, mat_qkv, preferred_element_type=jnp.float32) + vec_qkv).astype(
        jnp.bfloat16
    )
    queries = qkv_all[:, :model_width].reshape(slot_total, tok_dev, H, HD)
    keys_own = qkv_all[:, model_width : 2 * model_width].reshape(slot_total, tok_dev, model_width)
    values_own = qkv_all[:, 2 * model_width :].reshape(slot_total, tok_dev, model_width)
    keys_all, values_all = (
        lax.all_gather(keys_own, "seq", axis=1, tiled=True),
        lax.all_gather(values_own, "seq", axis=1, tiled=True),
    )
    keys_heads = keys_all.reshape(slot_total, -1, H, HD)
    values_heads = values_all.reshape(slot_total, -1, H, HD)
    scores = (
        jnp.einsum("sqhd,skhd->shqk", queries, keys_heads, preferred_element_type=jnp.float32)
        * scale
    )
    row_max = jnp.max(scores, axis=-1, keepdims=True)
    row_total = jnp.sum(jnp.exp(scores - row_max), axis=-1, keepdims=True)
    attn_probs = jnp.exp(scores - row_max) / row_total
    probs_b = attn_probs.astype(jnp.bfloat16)
    attended = jnp.einsum(
        "shqk,skhd->sqhd", probs_b, values_heads, preferred_element_type=jnp.float32
    )
    attended_b = attended.reshape(row_count, model_width).astype(jnp.bfloat16)
    mat_out, vec_out = collect(out_weight, out_bias)
    branch_att = (
        jnp.dot(attended_b, mat_out, preferred_element_type=jnp.float32) + vec_out
    ).reshape(slot_total, tok_dev, model_width)
    middle = latents + gate_att * branch_att
    normed_mlp, spread_mlp = normalize(middle)
    mlp_in = (
        (normed_mlp * (1.0 + scale_mlp) + shift_mlp)
        .astype(jnp.bfloat16)
        .reshape(row_count, model_width)
    )
    mat_up, vec_up = collect(up_weight, up_bias)
    hidden = jnp.dot(mlp_in, mat_up, preferred_element_type=jnp.float32) + vec_up
    activated = gelu_tanh(hidden).astype(jnp.bfloat16)
    mat_down, vec_down = collect(down_weight, down_bias)
    branch_mlp = (
        jnp.dot(activated, mat_down, preferred_element_type=jnp.float32) + vec_down
    ).reshape(slot_total, tok_dev, model_width)
    block_output = jnp.where(live_mask, middle + gate_mlp * branch_mlp, 0.0)
    mat_down = collect_again(down_weight)
    back_down = upstream * gate_mlp
    back_down_b = back_down.astype(jnp.bfloat16).reshape(row_count, model_width)
    grad_downw = spread_grad(activated, back_down_b)
    sum_downb = jnp.sum(back_down, axis=(0, 1))
    back_hidden = jnp.einsum(
        "rd,fd->rf", back_down_b, mat_down, preferred_element_type=jnp.float32
    ) * gelu_slope(hidden)
    back_hidden_b = back_hidden.astype(jnp.bfloat16)
    mat_up = collect_again(up_weight)
    grad_upw = spread_grad(mlp_in, back_hidden_b)
    sum_upb = jnp.sum(back_hidden, axis=0)
    back_mlp_in = jnp.einsum(
        "rf,cf->rc", back_hidden_b, mat_up, preferred_element_type=jnp.float32
    ).reshape(slot_total, tok_dev, model_width)
    back_middle = upstream + norm_back(back_mlp_in * (1.0 + scale_mlp), normed_mlp, spread_mlp)
    back_att = back_middle * gate_att
    back_att_b = back_att.astype(jnp.bfloat16).reshape(row_count, model_width)
    mat_out = collect_again(out_weight)
    grad_outw = spread_grad(attended_b, back_att_b)
    sum_outb = jnp.sum(back_att, axis=(0, 1))
    back_attended = jnp.einsum(
        "rd,cd->rc", back_att_b, mat_out, preferred_element_type=jnp.float32
    ).astype(jnp.bfloat16)
    back_attended = back_attended.reshape(slot_total, tok_dev, H, HD)
    back_probs = jnp.einsum(
        "sqhd,skhd->shqk", back_attended, values_heads, preferred_element_type=jnp.float32
    )
    row_delta = jnp.einsum("sqhd,sqhd->shq", back_attended.astype(jnp.float32), attended)[..., None]
    back_scores = (attn_probs * (back_probs - row_delta) * scale).astype(jnp.bfloat16)
    back_queries = jnp.einsum(
        "shqk,skhd->sqhd", back_scores, keys_heads, preferred_element_type=jnp.float32
    )
    key_terms = jnp.einsum(
        "shqk,sqhd->skhd", back_scores, queries, preferred_element_type=jnp.float32
    ).reshape(slot_total, -1, model_width)
    value_terms = jnp.einsum(
        "shqk,sqhd->skhd", probs_b, back_attended, preferred_element_type=jnp.float32
    ).reshape(slot_total, -1, model_width)
    back_keys, back_values = (
        lax.psum_scatter(key_terms, "seq", scatter_dimension=1, tiled=True),
        lax.psum_scatter(value_terms, "seq", scatter_dimension=1, tiled=True),
    )
    back_qkv = jnp.concatenate(
        [
            back_queries.reshape(row_count, model_width),
            back_keys.reshape(row_count, model_width),
            back_values.reshape(row_count, model_width),
        ],
        axis=1,
    )
    back_qkv_b = back_qkv.astype(jnp.bfloat16)
    mat_qkv = collect_again(qkv_weight)
    grad_qkvw = spread_grad(attn_in, back_qkv_b)
    sum_qkvb = jnp.sum(back_qkv, axis=0)
    back_attn_in = jnp.einsum(
        "rd,cd->rc", back_qkv_b, mat_qkv, preferred_element_type=jnp.float32
    ).reshape(slot_total, tok_dev, model_width)
    latent_gradient = jnp.where(
        live_mask,
        back_middle + norm_back(back_attn_in * (1.0 + scale_att), normed_att, spread_att),
        0.0,
    )
    slot_modgrad = jnp.concatenate(
        [
            jnp.sum(back_attn_in, axis=1),
            jnp.sum(back_attn_in * normed_att, axis=1),
            jnp.sum(back_middle * branch_att, axis=1),
            jnp.sum(back_mlp_in, axis=1),
            jnp.sum(back_mlp_in * normed_mlp, axis=1),
            jnp.sum(upstream * branch_mlp, axis=1),
        ],
        axis=1,
    )
    modgrad_table = jnp.dot(slot_matches.T, slot_modgrad, precision=lax.Precision.HIGHEST)
    modgrad_cols = lax.psum_scatter(modgrad_table, ("dp", "seq"), scatter_dimension=1, tiled=True)
    grad_adaw = jnp.dot(
        rounded(jax.nn.silu(condition)).T, modgrad_cols, precision=lax.Precision.HIGHEST
    )
    grad_adab = jnp.sum(modgrad_cols, axis=0)
    cond_term = jnp.dot(modgrad_cols, rounded(ada_weight).T, precision=lax.Precision.HIGHEST)
    cond_sum, total_qkvb, total_outb, total_upb, total_downb = lax.psum(
        (cond_term, sum_qkvb, sum_outb, sum_upb, sum_downb), ("dp", "seq")
    )
    condition_grad = cond_sum * silu_slope(condition)
    seq_index = lax.axis_index("seq")

    def own_part(full_sum, local_bias):
        length = local_bias.shape[0]
        return lax.dynamic_slice_in_dim(full_sum, seq_index * length, length)

    grad_qkvb = own_part(total_qkvb, qkv_bias)
    grad_outb = own_part(total_outb, out_bias)
    grad_upb = own_part(total_upb, up_bias)
    grad_downb = own_part(total_downb, down_bias)
    grads_all = (
        grad_adaw,
        grad_adab,
        grad_qkvw,
        grad_qkvb,
        grad_outw,
        grad_outb,
        grad_upw,
        grad_upb,
        grad_downw,
        grad_downb,
    )
    params_all = (
        ada_weight,
        ada_bias,
        qkv_weight,
        qkv_bias,
        out_weight,
        out_bias,
        up_weight,
        up_bias,
        down_weight,
        down_bias,
    )
    means_all = (
        mean_adaw,
        mean_adab,
        mean_qkvw,
        mean_qkvb,
        mean_outw,
        mean_outb,
        mean_upw,
        mean_upb,
        mean_downw,
        mean_downb,
    )
    squares_all = (
        sqmean_adaw,
        sqmean_adab,
        sqmean_qkvw,
        sqmean_qkvb,
        sqmean_outw,
        sqmean_outb,
        sqmean_upw,
        sqmean_upb,
        sqmean_downw,
        sqmean_downb,
    )
    updates = [
        adamw_step(p_item, g_item, m_item, v_item)
        for p_item, g_item, m_item, v_item in zip(params_all, grads_all, means_all, squares_all)
    ]
    newvals = tuple((entry[0] for entry in updates))
    newmeans = tuple((entry[1] for entry in updates))
    newsqrs = tuple((entry[2] for entry in updates))
    return (
        (block_output, latent_gradient, condition_grad) + grads_all + newvals + newmeans + newsqrs
    )


def solution(mesh):
    return jax.shard_map(
        on_device,
        mesh=mesh,
        in_specs=(
            P("dp", "seq", None),
            P(),
            P("dp", None),
            P("dp"),
            P("dp", "seq", None),
            P(None, ("dp", "seq")),
            P(("dp", "seq")),
            P("dp", "seq"),
            P("seq"),
            P("dp", "seq"),
            P("seq"),
            P("dp", "seq"),
            P("seq"),
            P("dp", "seq"),
            P("seq"),
            P(None, ("dp", "seq")),
            P(("dp", "seq")),
            P("dp", "seq"),
            P("seq"),
            P("dp", "seq"),
            P("seq"),
            P("dp", "seq"),
            P("seq"),
            P("dp", "seq"),
            P("seq"),
            P(None, ("dp", "seq")),
            P(("dp", "seq")),
            P("dp", "seq"),
            P("seq"),
            P("dp", "seq"),
            P("seq"),
            P("dp", "seq"),
            P("seq"),
            P("dp", "seq"),
            P("seq"),
        ),
        out_specs=(
            P("dp", "seq", None),
            P("dp", "seq", None),
            P(),
            P(None, ("dp", "seq")),
            P(("dp", "seq")),
            P("dp", "seq"),
            P("seq"),
            P("dp", "seq"),
            P("seq"),
            P("dp", "seq"),
            P("seq"),
            P("dp", "seq"),
            P("seq"),
            P(None, ("dp", "seq")),
            P(("dp", "seq")),
            P("dp", "seq"),
            P("seq"),
            P("dp", "seq"),
            P("seq"),
            P("dp", "seq"),
            P("seq"),
            P("dp", "seq"),
            P("seq"),
            P(None, ("dp", "seq")),
            P(("dp", "seq")),
            P("dp", "seq"),
            P("seq"),
            P("dp", "seq"),
            P("seq"),
            P("dp", "seq"),
            P("seq"),
            P("dp", "seq"),
            P("seq"),
            P(None, ("dp", "seq")),
            P(("dp", "seq")),
            P("dp", "seq"),
            P("seq"),
            P("dp", "seq"),
            P("seq"),
            P("dp", "seq"),
            P("seq"),
            P("dp", "seq"),
            P("seq"),
        ),
        check_vma=False,
    )
```

profile of v0, /device:TPU:0, one launch (start us, length us, event | category | flops | bytes accessed | tf_op | source)
XLA Modules:
  0.0 1488.1 jit_solution(5045543389649155626)
XLA Ops:
  8.4 10.0 all-gather.3
  20.1 5.4 all-gather.4
  26.6 8.7 all_gather.62
  37.1 70.0 %all-gather.2 = f32[32,216,8]{1,2,0:T(8,128)S(1)} all-gather(f32[1,216,8]{1,2,0:T(8,128)S(1)} %fusion.10), channel_id=1, replica_groups=mesh['dp'=16,'seq'=2] {'dp','seq'}, dimensions={0}, use_global_device_ids=true | all-gather | bytes 228096 | tf_op jit(solution)/shard_map/all_gather | solution.py:134
  111.4 7.3 all-reduce.7
  118.7 4.4 all-gather.5
  125.1 4.8 fusion.1
  129.9 7.7 all-gather
  139.6 8.0 all-gather.1
  157.0 71.1 %all-gather.16.cloned.1.call-done = bf16[1152,4608]{1,0:T(8,128)(2,1)} async-done(((bf16[72,4608]{1,0:T(8,128)(2,1)}), bf16[1152,4608]{1,0:T(8,128)(2,1)}) %all-gather.16.cloned.1.call-update) | async-done | bytes 10616848 | tf_op jit(solution)/shard_map/all_gather | solution.py:70
  228.0 5.9 convolution_add_fusion
  233.9 8.7 fusion.45
  242.7 211.9 %reduce-scatter.30.cloned.1.call-done = f32[288,1152]{1,0:T(8,128)} async-done(((f32[4608,1152]{1,0:T(8,128)}), f32[288,1152]{1,0:T(8,128)}) %reduce-scatter.30.cloned.1.call-update) | async-done | bytes 1327120 | tf_op jit(solution)/shard_map/reduce_scatter | solution.py:80
  457.8 27.5 %reduce-scatter.36.cloned.1.call-done = f32[576,288]{1,0:T(8,128)} async-done(((f32[1152,288]{1,0:T(8,128)}), f32[576,288]{1,0:T(8,128)}) %reduce-scatter.36.cloned.1.call-update) | async-done | bytes 663568
  491.3 10.8 all-gather.6
  507.9 87.0 %all-gather.18.cloned.1.call-done = bf16[4608,1152]{1,0:T(8,128)(2,1)} async-done(((bf16[288,1152]{1,0:T(8,128)(2,1)}), bf16[4608,1152]{1,0:T(8,128)(2,1)}) %all-gather.18.cloned.1.call-update) | async-done | bytes 10616848 | tf_op jit(solution)/shard_map/all_gather | solution.py:70
  594.9 8.7 fusion.95
  603.7 8.6 fusion.17
  625.1 15.3 %reduce-scatter.24.cloned.1.call-done = f32[1,128,1152]{1,2,0:T(8,128)} async-done(((f32[1,256,1152]{1,2,0:T(8,128)}), f32[1,128,1152]{1,2,0:T(8,128)}) %reduce-scatter.24.cloned.1.call-update) | async-done | bytes 589840 | tf_op jit(solution)/shard_map/reduce_scatter | solution.py:229
  640.4 24.1 %reduce-scatter.22.cloned.1.call-done = f32[1,128,1152]{1,2,0:T(8,128)} async-done(((f32[1,256,1152]{1,2,0:T(8,128)}), f32[1,128,1152]{1,2,0:T(8,128)}) %reduce-scatter.22.cloned.1.call-update) | async-done | bytes 589840 | tf_op jit(solution)/shard_map/reduce_scatter | solution.py:228
  664.6 6.8 fusion.19
  677.5 9.1 fusion.71
  686.7 11.5 fusion.29
  700.4 97.5 %all-reduce.11.cloned.1.call-done = f32[8,6912]{1,0:T(8,128)} async-done(((f32[8,6912]{1,0:T(8,128)}), f32[8,6912]{1,0:T(8,128)}) %all-reduce.11.cloned.1.call-update) | async-done | bytes 221200
  800.0 80.8 %reduce-scatter.40.cloned.1.call-done = f32[72,1152]{1,0:T(8,128)} async-done(((f32[1152,1152]{1,0:T(8,128)}), f32[72,1152]{1,0:T(8,128)}) %reduce-scatter.40.cloned.1.call-update) | async-done | bytes 331792
  883.0 171.3 %reduce-scatter.38.cloned.1.call-done = f32[72,3456]{1,0:T(8,128)} async-done(((f32[1152,3456]{1,0:T(8,128)}), f32[72,3456]{1,0:T(8,128)}) %reduce-scatter.38.cloned.1.call-update) | async-done | bytes 995344
  1059.4 211.5 %reduce-scatter.26.cloned.1.call-done = f32[72,4608]{1,0:T(8,128)} async-done(((f32[1152,4608]{1,0:T(8,128)}), f32[72,4608]{1,0:T(8,128)}) %reduce-scatter.26.cloned.1.call-update) | async-done | bytes 1327120 | tf_op jit(solution)/shard_map/reduce_scatter | solution.py:80
  1271.7 4.9 divide_subtract_fusion
  1276.6 125.8 %all-reduce.13.cloned.1.call-done = (f32[8,1152]{1,0:T(8,128)}, f32[3456]{0:T(1024)}, f32[1152]{0:T(1024)}, f32[4608]{0:T(1024)}, f32[1152]{0:T(1024)}) async-done(((f32[8,1152]{1,0:T(8,128)}, f32[3456]{0:T(1024)}, f32[1152]{0:T(1024)}, f32[4608]{0:T(1024)}, f32[1152]{0:T(1024)}), (f32[8,1152]{1,0:T(8,128)}, f32[3456]{0:T(1024)}, f32[1152]{0:T(1024)}, f32[4608]{0:T(1024)}, ...) | async-done | bytes 78352 | tf_op jit(solution)/shard_map/psum | solution.py:269
  1409.5 12.6 reduce-scatter.34.cloned.1.call-done
  1424.1 28.4 %reduce-scatter.32.cloned.1.call-done = f32[1728,72]{1,0:T(8,128)} async-done(((f32[3456,72]{1,0:T(8,128)}), f32[1728,72]{1,0:T(8,128)}) %reduce-scatter.32.cloned.1.call-update) | async-done | bytes 497680
  1456.9 21.8 %reduce-scatter.28.cloned.1.call-done = f32[72,2304]{1,0:T(8,128)} async-done(((f32[72,4608]{1,0:T(8,128)}), f32[72,2304]{1,0:T(8,128)}) %reduce-scatter.28.cloned.1.call-update) | async-done | bytes 663568 | tf_op jit(solution)/shard_map/reduce_scatter | solution.py:81
  (304 shorter events, 82.2 us)
Async XLA Ops:
  7.2 117.8 %all-gather.12.cloned.1.call-start = ((), (), s32[]{:S(2)}) async-start(), calls=%async_computation.10 | async-start | bytes 8460288 | tf_op jit(solution)/shard_map/all_gather | solution.py:70
  20.0 132.9 %all-gather.14.cloned.1.call-start = ((), (), s32[]{:S(2)}) async-start(), calls=%async_computation.11 | async-start | bytes 2820096 | tf_op jit(solution)/shard_map/all_gather | solution.py:70
  26.4 201.6 %all-gather.16.cloned.1.call-start = ((), (), s32[]{:S(2)}) async-start(), calls=%async_computation.12 | async-start | bytes 11280384 | tf_op jit(solution)/shard_map/all_gather | solution.py:70
  35.3 419.3 %reduce-scatter.30.cloned.1.call-start = ((), (), s32[]{:S(2)}) async-start(), calls=%async_computation.18 | async-start | bytes 22560768 | tf_op jit(solution)/shard_map/reduce_scatter | solution.py:80
  242.7 242.7 %reduce-scatter.36.cloned.1.call-start = ((), (), s32[]{:S(2)}) async-start(), calls=%async_computation.21 | async-start | bytes 2654208
  457.8 137.1 %all-gather.18.cloned.1.call-start = ((), (), s32[]{:S(2)}) async-start(), calls=%async_computation.13 | async-start | bytes 11280384 | tf_op jit(solution)/shard_map/all_gather | solution.py:70
  506.4 134.0 %reduce-scatter.24.cloned.1.call-start = ((), (), s32[]{:S(2)}) async-start(), calls=%async_computation.15 | async-start | bytes 1769472 | tf_op jit(solution)/shard_map/reduce_scatter | solution.py:229
  620.2 44.3 %reduce-scatter.22.cloned.1.call-start = ((), (), s32[]{:S(2)}) async-start(), calls=%async_computation.14 | async-start | bytes 1769472 | tf_op jit(solution)/shard_map/reduce_scatter | solution.py:228
  624.5 173.3 %all-reduce.11.cloned.1.call-start = ((), (), s32[]{:S(2)}) async-start(), calls=%async_computation.22 | async-start | bytes 442368
  673.0 207.8 %reduce-scatter.40.cloned.1.call-start = ((), (), s32[]{:S(2)}) async-start(), calls=%async_computation.24 | async-start | bytes 5640192
  676.5 377.8 %reduce-scatter.38.cloned.1.call-start = ((), (), s32[]{:S(2)}) async-start(), calls=%async_computation.23 | async-start | bytes 16920576
  686.7 584.2 %reduce-scatter.26.cloned.1.call-start = ((), (), s32[]{:S(2)}) async-start(), calls=%async_computation.16 | async-start | bytes 22560768 | tf_op jit(solution)/shard_map/reduce_scatter | solution.py:80
  698.2 704.2 %all-reduce.13.cloned.1.call-start = ((), (), s32[]{:S(2)}) async-start(), calls=%async_computation.25 | async-start | bytes 180224 | tf_op jit(solution)/shard_map/psum | solution.py:269
  799.9 622.1 %reduce-scatter.34.cloned.1.call-start = ((), (), s32[]{:S(2)}) async-start(), calls=%async_computation.20 | async-start | bytes 884736
  882.9 174.6 %copy-start.82 = (f32[128]{0:T(128)S(1)}, f32[128]{0:T(128)}, u32[]{:S(2)}) copy-start(f32[128]{0:T(128)} %get-tuple-element.46) | copy-start | bytes 1540
  882.9 174.6 %copy-start.83 = (f32[128]{0:T(128)S(1)}, f32[128]{0:T(128)}, u32[]{:S(2)}) copy-start(f32[128]{0:T(128)} %get-tuple-element.54) | copy-start | bytes 1540
  882.9 174.6 %copy-start.57 = (f32[128]{0:T(128)S(1)}, f32[128]{0:T(128)}, u32[]{:S(2)}) copy-start(f32[128]{0:T(128)} %copy-done.55) | copy-start | bytes 1540
  882.9 174.6 %copy-start.61 = (f32[128]{0:T(128)S(1)}, f32[128]{0:T(128)}, u32[]{:S(2)}) copy-start(f32[128]{0:T(128)} %copy-done.59) | copy-start | bytes 1540
  882.9 569.6 %reduce-scatter.32.cloned.1.call-start = ((), (), s32[]{:S(2)}) async-start(), calls=%async_computation.19 | async-start | bytes 2654208
  1057.3 213.6 %copy-start.79 = (f32[216]{0:T(256)S(1)}, f32[216]{0:T(256)}, u32[]{:S(2)}) copy-start(f32[216]{0:T(256)} %param.41) | copy-start | bytes 2596
  1057.3 213.6 %copy-start.80 = (f32[216]{0:T(256)S(1)}, f32[216]{0:T(256)}, u32[]{:S(2)}) copy-start(f32[216]{0:T(256)} %param.51) | copy-start | bytes 2596
  1057.3 213.6 %copy-start.81 = (f32[216]{0:T(256)S(1)}, f32[216]{0:T(256)}, u32[]{:S(2)}) copy-start(f32[216]{0:T(256)} %param.61) | copy-start | bytes 2596
  1057.3 214.2 %copy-start.14 = (f32[1152,216]{0,1:T(8,128)S(1)}, f32[1152,216]{0,1:T(8,128)}, u32[]{:S(2)}) copy-start(f32[1152,216]{0,1:T(8,128)} %param.40) | copy-start | bytes 2985988
  1057.3 214.2 %copy-start.36 = (bf16[8,1152]{1,0:T(8,128)(2,1)S(1)}, bf16[8,1152]{1,0:T(8,128)(2,1)}, u32[]{:S(2)}) copy-start(bf16[8,1152]{1,0:T(8,128)(2,1)} %copy-done.35) | copy-start | bytes 55300
  1057.4 421.3 %reduce-scatter.28.cloned.1.call-start = ((), (), s32[]{:S(2)}) async-start(), calls=%async_computation.17 | async-start | bytes 1990656 | tf_op jit(solution)/shard_map/reduce_scatter | solution.py:81
  1059.4 217.2 %copy-start.73 = (f32[216]{0:T(256)}, f32[216]{0:T(256)S(1)}, u32[]{:S(2)}) copy-start(f32[216]{0:T(256)S(1)} %dynamic-slice_reduce_fusion) | copy-start | bytes 2596
  1271.6 135.0 %copy-start.44 = (f32[2304]{0:T(1024)S(1)}, f32[2304]{0:T(1024)}, u32[]{:S(2)}) copy-start(f32[2304]{0:T(1024)} %param.47) | copy-start | bytes 27652
  1271.7 136.4 %copy-start.38 = (f32[8,1152]{1,0:T(8,128)S(1)}, f32[8,1152]{1,0:T(8,128)}, u32[]{:S(2)}) copy-start(f32[8,1152]{1,0:T(8,128)} %param.36) | copy-start | bytes 110596
  1271.7 151.5 %copy-start.26 = (f32[72,576]{1,0:T(8,128)S(1)}, f32[72,576]{1,0:T(8,128)}, u32[]{:S(2)}) copy-start(f32[72,576]{1,0:T(8,128)} %param.44) | copy-start | bytes 497668
  1271.7 151.5 %copy-start.33 = (f32[72,576]{1,0:T(8,128)S(1)}, f32[72,576]{1,0:T(8,128)}, u32[]{:S(2)}) copy-start(f32[72,576]{1,0:T(8,128)} %param.54) | copy-start | bytes 497668
  1271.7 151.5 %copy-start.34 = (f32[72,576]{1,0:T(8,128)S(1)}, f32[72,576]{1,0:T(8,128)}, u32[]{:S(2)}) copy-start(f32[72,576]{1,0:T(8,128)} %param.64) | copy-start | bytes 497668
  1276.6 177.6 %copy-start.23 = (f32[72,1728]{1,0:T(8,128)S(1)}, f32[72,1728]{1,0:T(8,128)}, u32[]{:S(2)}) copy-start(f32[72,1728]{1,0:T(8,128)} %param.42) | copy-start | bytes 1492996
  (72 other events, 2595.4 us)
Sparse Core Ops, SparseCore 0:
  20.1 73.9 all-gather.11
  96.8 41.6 all-gather.13
  140.8 87.1 all-gather.15
  242.8 211.8 reduce-scatter.29
  457.9 27.4 reduce-scatter.35
  506.5 88.3 all-gather.17
  620.3 20.0 reduce-scatter.23
  642.6 21.8 reduce-scatter.21
  673.1 124.6 all-reduce.10
  801.7 79.0 reduce-scatter.39
  885.0 169.3 reduce-scatter.37
  1058.3 212.5 reduce-scatter.25
  1279.0 123.3 all-reduce.12
  1405.1 16.9 reduce-scatter.33
  1424.2 28.3 reduce-scatter.31
  1455.2 23.4 reduce-scatter.27
where the time goes:
time: 1490 us
  waiting for transfers between devices  1190 us (80%)
  blocking collectives  132 us (9%)
  matrix products  92 us (6%)
  local copies, waits for them, and re-layouts  30.4 us (2%)
  other arithmetic  27.4 us (2%)
  between operations  18 us (1%)
    reduce_scatter x2, waiting for transfers between devices, spread_grad(): lax.psum_scatter(term, 'dp', scatter_dimension=0, tiled=True)  423 us
    unnamed x22, waiting for transfers between devices  418 us
    all_gather x4, waiting for transfers between devices, collect(): lax.all_gather(pieces, 'dp', axis=0, tiled=True)  158 us
    psum x1, waiting for transfers between devices, on_device(): lax.psum((cond_term, sum_qkvb, sum_outb, sum_upb, sum_downb), ('dp', 'seq'))  126 us
    all_gather x1, blocking collectives, on_device(): modulation = lax.all_gather(mod_cols, ('dp', 'seq'), axis=1, tiled=True)  70 us
    all_gather x4, blocking collectives, collect(): lax.all_gather(weight.astype(jnp.bfloat16), 'seq', axis=1, tiled=True)  34.8 us
    dot_general x4, matrix products, spread_grad(): jnp.einsum('rc,rd->cd', left, right, preferred_element_type=jnp.float32)  32.5 us
  transfers between devices with their start and end apart: 16, of which 14 were waited for; matrix products, arithmetic and copies ran while one was open for 5% of the time, Pallas kernels for 0%

commit v1 on v0

--- a/solution.py
+++ b/solution.py
@@ -266,8 +266,14 @@
     )
     grad_adab = jnp.sum(modgrad_cols, axis=0)
     cond_term = jnp.dot(modgrad_cols, rounded(ada_weight).T, precision=lax.Precision.HIGHEST)
-    cond_sum, total_qkvb, total_outb, total_upb, total_downb = lax.psum(
-        (cond_term, sum_qkvb, sum_outb, sum_upb, sum_downb), ("dp", "seq")
+
+    def members_all_compute(incoming_x, across, group_axis):
+        for b in (across, group_axis):
+            incoming_x = lax.psum(incoming_x, axis_name=b)
+        return incoming_x
+
+    cond_sum, total_qkvb, total_outb, total_upb, total_downb = members_all_compute(
+        (cond_term, sum_qkvb, sum_outb, sum_upb, sum_downb), "seq", group_axis="dp"
     )
     condition_grad = cond_sum * silu_slope(condition)
     seq_index = lax.axis_index("seq")

time: 1490 us -> 1490 us (level)
  waiting for transfers between devices: 1190 us -> 1170 us
    psum x1 -> x2, waiting for transfers between devices: 126 us -> 86 us  [members_all_compute(): incoming_x = lax.psum(incoming_x, axis_name=b)]
    unnamed x22 -> x23, waiting for transfers between devices: 418 us -> 443 us
  transfers between devices with their start and end apart: 16 -> 17, of which waited for: 14 -> 14; matrix products, arithmetic and copies ran while one was open for 5% -> 5% of each run, Pallas kernels for 0% -> 0%
where the time goes in v1:
time: 1490 us; the launch traced here: 1480 us
  waiting for transfers between devices  1170 us (79%)
  blocking collectives  132 us (9%)
  matrix products  92.9 us (6%)
  local copies, waits for them, and re-layouts  32.5 us (2%)
  other arithmetic  31.1 us (2%)
  between operations  17.9 us (1%)
    unnamed x23, waiting for transfers between devices  443 us
    reduce_scatter x2, waiting for transfers between devices, spread_grad(): lax.psum_scatter(term, 'dp', scatter_dimension=0, tiled=True)  424 us
    all_gather x4, waiting for transfers between devices, collect(): lax.all_gather(pieces, 'dp', axis=0, tiled=True)  158 us
    psum x2, waiting for transfers between devices, members_all_compute(): incoming_x = lax.psum(incoming_x, axis_name=b)  86 us
    all_gather x1, blocking collectives, on_device(): modulation = lax.all_gather(mod_cols, ('dp', 'seq'), axis=1, tiled=True)  70 us
    all_gather x4, blocking collectives, collect(): lax.all_gather(weight.astype(jnp.bfloat16), 'seq', axis=1, tiled=True)  34.9 us
    dot_general x4, matrix products, spread_grad(): jnp.einsum('rc,rd->cd', left, right, preferred_element_type=jnp.float32)  33.3 us
  transfers between devices with their start and end apart: 17, of which 14 were waited for; matrix products, arithmetic and copies ran while one was open for 5% of the time, Pallas kernels for 0%

profile of v1, /device:TPU:0, one launch (start us, length us, event | category | flops | bytes accessed | tf_op | source)
XLA Modules:
  0.0 1479.4 jit_solution(5996209003588449208)
XLA Ops:
  8.4 10.0 all-gather.3
  20.1 5.4 all-gather.4
  26.6 8.7 all_gather.62
  37.1 70.0 %all-gather.2 = f32[32,216,8]{1,2,0:T(8,128)S(1)} all-gather(f32[1,216,8]{1,2,0:T(8,128)S(1)} %fusion.10), channel_id=1, replica_groups=mesh['dp'=16,'seq'=2] {'dp','seq'}, dimensions={0}, use_global_device_ids=true | all-gather | bytes 228096 | tf_op jit(solution)/shard_map/all_gather | solution.py:134
  111.4 7.3 all-reduce.8
  118.7 4.4 all-gather.5
  125.1 4.8 fusion.1
  129.9 7.7 all-gather
  139.6 8.0 all-gather.1
  157.0 71.1 %all-gather.16.cloned.1.call-done = bf16[1152,4608]{1,0:T(8,128)(2,1)} async-done(((bf16[72,4608]{1,0:T(8,128)(2,1)}), bf16[1152,4608]{1,0:T(8,128)(2,1)}) %all-gather.16.cloned.1.call-update) | async-done | bytes 10616848 | tf_op jit(solution)/shard_map/all_gather | solution.py:70
  228.0 5.9 convolution_add_fusion
  233.9 8.7 fusion.45
  242.7 211.9 %reduce-scatter.30.cloned.1.call-done = f32[288,1152]{1,0:T(8,128)} async-done(((f32[4608,1152]{1,0:T(8,128)}), f32[288,1152]{1,0:T(8,128)}) %reduce-scatter.30.cloned.1.call-update) | async-done | bytes 1327120 | tf_op jit(solution)/shard_map/reduce_scatter | solution.py:80
  457.8 27.5 %reduce-scatter.36.cloned.1.call-done = f32[576,288]{1,0:T(8,128)} async-done(((f32[1152,288]{1,0:T(8,128)}), f32[576,288]{1,0:T(8,128)}) %reduce-scatter.36.cloned.1.call-update) | async-done | bytes 663568
  491.3 10.8 all-gather.6
  507.9 87.0 %all-gather.18.cloned.1.call-done = bf16[4608,1152]{1,0:T(8,128)(2,1)} async-done(((bf16[288,1152]{1,0:T(8,128)(2,1)}), bf16[4608,1152]{1,0:T(8,128)(2,1)}) %all-gather.18.cloned.1.call-update) | async-done | bytes 10616848 | tf_op jit(solution)/shard_map/all_gather | solution.py:70
  594.9 8.7 fusion.95
  603.7 8.6 fusion.17
  625.5 14.8 %reduce-scatter.24.cloned.1.call-done = f32[1,128,1152]{1,2,0:T(8,128)} async-done(((f32[1,256,1152]{1,2,0:T(8,128)}), f32[1,128,1152]{1,2,0:T(8,128)}) %reduce-scatter.24.cloned.1.call-update) | async-done | bytes 589840 | tf_op jit(solution)/shard_map/reduce_scatter | solution.py:229
  640.3 24.1 %reduce-scatter.22.cloned.1.call-done = f32[1,128,1152]{1,2,0:T(8,128)} async-done(((f32[1,256,1152]{1,2,0:T(8,128)}), f32[1,128,1152]{1,2,0:T(8,128)}) %reduce-scatter.22.cloned.1.call-update) | async-done | bytes 589840 | tf_op jit(solution)/shard_map/reduce_scatter | solution.py:228
  664.5 6.8 fusion.19
  681.0 122.4 %all-reduce.13.cloned.1.call-done = f32[8,6912]{1,0:T(8,128)} async-done(((f32[8,6912]{1,0:T(8,128)}), f32[8,6912]{1,0:T(8,128)}) %all-reduce.13.cloned.1.call-update) | async-done | bytes 221200
  809.7 9.1 fusion.71
  819.5 11.4 fusion.29
  831.5 81.3 %reduce-scatter.40.cloned.1.call-done = f32[72,1152]{1,0:T(8,128)} async-done(((f32[1152,1152]{1,0:T(8,128)}), f32[72,1152]{1,0:T(8,128)}) %reduce-scatter.40.cloned.1.call-update) | async-done | bytes 331792
  915.0 171.4 %reduce-scatter.38.cloned.1.call-done = f32[72,3456]{1,0:T(8,128)} async-done(((f32[1152,3456]{1,0:T(8,128)}), f32[72,3456]{1,0:T(8,128)}) %reduce-scatter.38.cloned.1.call-update) | async-done | bytes 995344
  1091.5 211.7 %reduce-scatter.26.cloned.1.call-done = f32[72,4608]{1,0:T(8,128)} async-done(((f32[1152,4608]{1,0:T(8,128)}), f32[72,4608]{1,0:T(8,128)}) %reduce-scatter.26.cloned.1.call-update) | async-done | bytes 1327120 | tf_op jit(solution)/shard_map/reduce_scatter | solution.py:80
  1304.0 4.9 divide_subtract_fusion
  1308.9 86.0 %all-reduce.15.cloned.1.call-done = (f32[8,1152]{1,0:T(8,128)}, f32[3456]{0:T(1024)}, f32[1152]{0:T(1024)}, f32[4608]{0:T(1024)}, f32[1152]{0:T(1024)}) async-done(((f32[8,1152]{1,0:T(8,128)}, f32[3456]{0:T(1024)}, f32[1152]{0:T(1024)}, f32[4608]{0:T(1024)}, f32[1152]{0:T(1024)}), (f32[8,1152]{1,0:T(8,128)}, f32[3456]{0:T(1024)}, f32[1152]{0:T(1024)}, f32[4608]{0:T(1024)}, ...) | async-done | bytes 78352 | tf_op jit(solution)/shard_map/psum | solution.py:272
  1402.0 11.4 reduce-scatter.34.cloned.1.call-done
  1415.4 28.4 %reduce-scatter.32.cloned.1.call-done = f32[1728,72]{1,0:T(8,128)} async-done(((f32[3456,72]{1,0:T(8,128)}), f32[1728,72]{1,0:T(8,128)}) %reduce-scatter.32.cloned.1.call-update) | async-done | bytes 497680
  1448.2 21.8 %reduce-scatter.28.cloned.1.call-done = f32[72,2304]{1,0:T(8,128)} async-done(((f32[72,4608]{1,0:T(8,128)}), f32[72,2304]{1,0:T(8,128)}) %reduce-scatter.28.cloned.1.call-update) | async-done | bytes 663568 | tf_op jit(solution)/shard_map/reduce_scatter | solution.py:81
  (303 shorter events, 89.5 us)
Async XLA Ops:
  7.2 117.8 %all-gather.12.cloned.1.call-start = ((), (), s32[]{:S(2)}) async-start(), calls=%async_computation.10 | async-start | bytes 8460288 | tf_op jit(solution)/shard_map/all_gather | solution.py:70
  20.0 132.9 %all-gather.14.cloned.1.call-start = ((), (), s32[]{:S(2)}) async-start(), calls=%async_computation.11 | async-start | bytes 2820096 | tf_op jit(solution)/shard_map/all_gather | solution.py:70
  26.4 201.6 %all-gather.16.cloned.1.call-start = ((), (), s32[]{:S(2)}) async-start(), calls=%async_computation.12 | async-start | bytes 11280384 | tf_op jit(solution)/shard_map/all_gather | solution.py:70
  35.3 419.3 %reduce-scatter.30.cloned.1.call-start = ((), (), s32[]{:S(2)}) async-start(), calls=%async_computation.18 | async-start | bytes 22560768 | tf_op jit(solution)/shard_map/reduce_scatter | solution.py:80
  242.7 242.6 %reduce-scatter.36.cloned.1.call-start = ((), (), s32[]{:S(2)}) async-start(), calls=%async_computation.21 | async-start | bytes 2654208
  457.8 137.1 %all-gather.18.cloned.1.call-start = ((), (), s32[]{:S(2)}) async-start(), calls=%async_computation.13 | async-start | bytes 11280384 | tf_op jit(solution)/shard_map/all_gather | solution.py:70
  506.3 134.0 %reduce-scatter.24.cloned.1.call-start = ((), (), s32[]{:S(2)}) async-start(), calls=%async_computation.15 | async-start | bytes 1769472 | tf_op jit(solution)/shard_map/reduce_scatter | solution.py:229
  620.1 44.3 %reduce-scatter.22.cloned.1.call-start = ((), (), s32[]{:S(2)}) async-start(), calls=%async_computation.14 | async-start | bytes 1769472 | tf_op jit(solution)/shard_map/reduce_scatter | solution.py:228
  624.5 178.9 %all-reduce.13.cloned.1.call-start = ((), (), s32[]{:S(2)}) async-start(), calls=%async_computation.22 | async-start | bytes 442368
  671.3 134.2 %copy-start.6 = (f32[1,128,1152]{2,1,0:T(8,128)S(1)}, f32[1,128,1152]{2,1,0:T(8,128)}, u32[]{:S(2)}) copy-start(f32[1,128,1152]{2,1,0:T(8,128)} %copy-done.5) | copy-start | bytes 1769476
  678.5 152.5 %all-reduce.17.cloned.1.call-start = ((), (), s32[]{:S(2)}) async-start(), calls=%async_computation.26 | async-start | bytes 180224 | tf_op jit(solution)/shard_map/psum | solution.py:272
  805.5 107.4 %reduce-scatter.40.cloned.1.call-start = ((), (), s32[]{:S(2)}) async-start(), calls=%async_computation.24 | async-start | bytes 5640192
  809.7 276.8 %reduce-scatter.38.cloned.1.call-start = ((), (), s32[]{:S(2)}) async-start(), calls=%async_computation.23 | async-start | bytes 16920576
  818.8 484.4 %reduce-scatter.26.cloned.1.call-start = ((), (), s32[]{:S(2)}) async-start(), calls=%async_computation.16 | async-start | bytes 22560768 | tf_op jit(solution)/shard_map/reduce_scatter | solution.py:80
  830.9 564.0 %all-reduce.15.cloned.1.call-start = ((), (), s32[]{:S(2)}) async-start(), calls=%async_computation.25 | async-start | bytes 180224 | tf_op jit(solution)/shard_map/psum | solution.py:272
  831.5 581.8 %reduce-scatter.34.cloned.1.call-start = ((), (), s32[]{:S(2)}) async-start(), calls=%async_computation.20 | async-start | bytes 884736
  914.9 174.7 %copy-start.80 = (f32[128]{0:T(128)S(1)}, f32[128]{0:T(128)}, u32[]{:S(2)}) copy-start(f32[128]{0:T(128)} %get-tuple-element.46) | copy-start | bytes 1540
  914.9 174.7 %copy-start.81 = (f32[128]{0:T(128)S(1)}, f32[128]{0:T(128)}, u32[]{:S(2)}) copy-start(f32[128]{0:T(128)} %get-tuple-element.54) | copy-start | bytes 1540
  914.9 174.7 %copy-start.55 = (f32[128]{0:T(128)S(1)}, f32[128]{0:T(128)}, u32[]{:S(2)}) copy-start(f32[128]{0:T(128)} %copy-done.54) | copy-start | bytes 1540
  914.9 174.7 %copy-start.59 = (f32[128]{0:T(128)S(1)}, f32[128]{0:T(128)}, u32[]{:S(2)}) copy-start(f32[128]{0:T(128)} %copy-done.58) | copy-start | bytes 1540
  914.9 528.9 %reduce-scatter.32.cloned.1.call-start = ((), (), s32[]{:S(2)}) async-start(), calls=%async_computation.19 | async-start | bytes 2654208
  1089.4 213.8 %copy-start.77 = (f32[216]{0:T(256)S(1)}, f32[216]{0:T(256)}, u32[]{:S(2)}) copy-start(f32[216]{0:T(256)} %param.41) | copy-start | bytes 2596
  1089.4 213.8 %copy-start.78 = (f32[216]{0:T(256)S(1)}, f32[216]{0:T(256)}, u32[]{:S(2)}) copy-start(f32[216]{0:T(256)} %param.51) | copy-start | bytes 2596
  1089.4 213.8 %copy-start.79 = (f32[216]{0:T(256)S(1)}, f32[216]{0:T(256)}, u32[]{:S(2)}) copy-start(f32[216]{0:T(256)} %param.61) | copy-start | bytes 2596
  1089.4 214.4 %copy-start.13 = (f32[1152,216]{0,1:T(8,128)S(1)}, f32[1152,216]{0,1:T(8,128)}, u32[]{:S(2)}) copy-start(f32[1152,216]{0,1:T(8,128)} %param.40) | copy-start | bytes 2985988
  1089.4 214.4 %copy-start.35 = (bf16[8,1152]{1,0:T(8,128)(2,1)S(1)}, bf16[8,1152]{1,0:T(8,128)(2,1)}, u32[]{:S(2)}) copy-start(bf16[8,1152]{1,0:T(8,128)(2,1)} %copy-done.34) | copy-start | bytes 55300
  1089.5 380.5 %reduce-scatter.28.cloned.1.call-start = ((), (), s32[]{:S(2)}) async-start(), calls=%async_computation.17 | async-start | bytes 1990656 | tf_op jit(solution)/shard_map/reduce_scatter | solution.py:81
  1091.5 217.4 %copy-start.71 = (f32[216]{0:T(256)}, f32[216]{0:T(256)S(1)}, u32[]{:S(2)}) copy-start(f32[216]{0:T(256)S(1)} %dynamic-slice_reduce_fusion) | copy-start | bytes 2596
  1304.0 110.5 %copy-start.24 = (f32[72,576]{1,0:T(8,128)S(1)}, f32[72,576]{1,0:T(8,128)}, u32[]{:S(2)}) copy-start(f32[72,576]{1,0:T(8,128)} %param.44) | copy-start | bytes 497668
  1304.0 110.4 %copy-start.32 = (f32[72,576]{1,0:T(8,128)S(1)}, f32[72,576]{1,0:T(8,128)}, u32[]{:S(2)}) copy-start(f32[72,576]{1,0:T(8,128)} %param.54) | copy-start | bytes 497668
  1304.0 110.4 %copy-start.33 = (f32[72,576]{1,0:T(8,128)S(1)}, f32[72,576]{1,0:T(8,128)}, u32[]{:S(2)}) copy-start(f32[72,576]{1,0:T(8,128)} %param.64) | copy-start | bytes 497668
  1308.9 136.5 %copy-start.21 = (f32[72,1728]{1,0:T(8,128)S(1)}, f32[72,1728]{1,0:T(8,128)}, u32[]{:S(2)}) copy-start(f32[72,1728]{1,0:T(8,128)} %param.42) | copy-start | bytes 1492996
  (71 other events, 2262.6 us)
Sparse Core Ops, SparseCore 0:
  20.1 73.9 all-gather.11
  96.8 41.6 all-gather.13
  140.8 87.1 all-gather.15
  242.8 211.8 reduce-scatter.29
  457.9 27.3 reduce-scatter.35
  506.5 88.3 all-gather.17
  620.2 20.0 reduce-scatter.23
  642.6 21.8 reduce-scatter.21
  678.6 124.6 all-reduce.12
  808.1 22.3 all-reduce.16
  834.5 78.2 reduce-scatter.39
  916.8 169.5 reduce-scatter.37
  1090.5 212.6 reduce-scatter.25
  1307.1 87.7 all-reduce.14
  1397.6 15.7 reduce-scatter.33
  1415.5 28.3 reduce-scatter.31
  1446.5 23.4 reduce-scatter.27
